TPU v7x, 32 devices: a whole 2x2x4 slice. The times are simulated.
32 devices in a mesh: seq: 8 (over z, core), fsdp: 4 (over y, x).
Axes of the slice: x: 2, y: 2, z: 4, core: 2. Of those that a mesh axis runs over, the one named last changes fastest.
Arguments:
- signal: bfloat16 [4, 8192, 1024], P('fsdp', 'seq'), may hold values from -6 to 6
- cotangent: bfloat16 [4, 8192, 1024], P('fsdp', 'seq'), may hold values from -6 to 6
- w_in: bfloat16 [1024, 1024], P('fsdp'), may hold values from -0.1875 to 0.1875
- w_conv: bfloat16 [2, 1024, 128], P(None, 'seq'), may hold values from -0.5 to 0.5
- w_out: bfloat16 [1024, 1024], P('fsdp'), may hold values from -0.1875 to 0.1875
- dilation: int32 [16], P('seq'), may hold values from 512 to 4095
- lengths: int32 [4], P('fsdp'), may hold values from 2048 to 8192, as said below
Outputs:
- grad_signal: bfloat16 [4, 8192, 1024], P('fsdp', 'seq')
- grad_in: float32 [1024, 1024], P('fsdp')
- grad_out: float32 [1024, 1024], P('fsdp')
- grad_conv: float32 [2, 1024, 128], P(None, 'seq')
Inputs may be any that keep to these rules, and one draw needn't show every extreme that they name: `lengths`: some record in every draw holds all 8192 samples.
All inputs are finite; a program needn't handle non-finite values.
Results may differ from a plain program's by a relative error of at most 0.0068.
Values may be sent and summed in bfloat16 or wider, within the bound.
No kernel may reach another device: no remote copies, remote signals or barrier semaphores. Data moves between devices by JAX's collectives and lax.ppermute only.
A program may use at most 128 MiB of HBM per device.

v0:
```python
import math
import jax
import jax.numpy as jnp
from jax import lax
from jax.sharding import PartitionSpec as P


def delayed(series, amount):
    padded = jnp.concatenate([jnp.zeros_like(series), series], axis=0)
    return lax.dynamic_slice_in_dim(padded, series.shape[0] - amount, series.shape[0], 0)


def advanced(series, amount):
    padded = jnp.concatenate([series, jnp.zeros_like(series)], axis=0)
    return lax.dynamic_slice_in_dim(padded, amount, series.shape[0], 0)


def group_pass(projected, grad_gated, kernel, amount, live_mask):
    group_width = kernel.shape[0] // 2
    stacked = jnp.concatenate([projected, delayed(projected, amount)], axis=1)
    pre_acts = jnp.dot(stacked, kernel, preferred_element_type=jnp.float32)
    tanh_act = jnp.tanh(pre_acts[:, :group_width])
    sig_act = jax.nn.sigmoid(pre_acts[:, group_width:])
    masked = live_mask[:, None]
    gated_out = (tanh_act * sig_act * masked).astype(jnp.bfloat16)
    grad_masked = grad_gated.astype(jnp.float32) * masked
    grad_filter = grad_masked * sig_act * (1.0 - tanh_act * tanh_act)
    grad_gate = grad_masked * tanh_act * sig_act * (1.0 - sig_act)
    grad_acts = jnp.concatenate([grad_filter, grad_gate], axis=1).astype(jnp.bfloat16)
    grad_kernel = jnp.dot(stacked.T, grad_acts, preferred_element_type=jnp.float32)
    paired = jnp.concatenate([grad_acts, advanced(grad_acts, amount)], axis=1)
    back_kernel = jnp.concatenate([kernel[:group_width].T, kernel[group_width:].T], axis=0)
    grad_mixed = jnp.dot(paired, back_kernel, preferred_element_type=jnp.float32).astype(
        jnp.bfloat16
    )
    return (gated_out, grad_mixed, grad_kernel)


def column_order(series, fsdp_size, seq_size):
    samples, channels = series.shape
    quarter = channels // (fsdp_size * seq_size)
    return (
        series.reshape(samples, fsdp_size, seq_size, quarter)
        .transpose(0, 2, 1, 3)
        .reshape(samples, channels)
    )


def outer_terms(left_side, right_side):
    return lax.dot_general(
        left_side, right_side, (((0,), (0,)), ((), ())), preferred_element_type=jnp.float32
    )


def local(signal, cotangent, w_in, w_conv, w_out, dilation, lengths):
    record = signal[0]
    upstream = cotangent[0]
    samples, channels = record.shape
    seq_size = lax.axis_size("seq")
    fsdp_size = lax.axis_size("fsdp")
    full_len = samples * seq_size
    local_groups = dilation.shape[0]
    local_chans = w_conv.shape[1]
    group_width = local_chans // local_groups
    factor = 1.0 / math.sqrt(full_len * fsdp_size)
    projected = jnp.dot(
        record, lax.all_gather(w_in, "fsdp", axis=0, tiled=True), preferred_element_type=jnp.float32
    ).astype(jnp.bfloat16)
    grad_gated = lax.dot_general(
        upstream,
        lax.all_gather(w_out, "fsdp", axis=0, tiled=True),
        (((1,), (1,)), ((), ())),
        preferred_element_type=jnp.float32,
    ).astype(jnp.bfloat16)
    proj_groups, grad_groups = (
        lax.all_to_all(projected, "seq", split_axis=1, concat_axis=0, tiled=True),
        lax.all_to_all(grad_gated, "seq", split_axis=1, concat_axis=0, tiled=True),
    )
    live_mask = (jnp.arange(full_len, dtype=jnp.int32) < lengths[0]).astype(jnp.float32)
    gated_parts = []
    mixed_parts = []
    tap_zero = []
    tap_one = []
    for group_index in range(local_groups):
        low_chan = group_index * group_width
        kernel = jnp.concatenate(
            [
                w_conv[0, low_chan : low_chan + group_width],
                w_conv[1, low_chan : low_chan + group_width],
            ],
            axis=0,
        )
        gated_out, grad_mixed, grad_kernel = group_pass(
            proj_groups[:, low_chan : low_chan + group_width],
            grad_groups[:, low_chan : low_chan + group_width],
            kernel,
            dilation[group_index],
            live_mask,
        )
        gated_parts.append(gated_out)
        mixed_parts.append(grad_mixed)
        tap_zero.append(grad_kernel[:group_width])
        tap_one.append(grad_kernel[group_width:])
    gated_groups = jnp.concatenate(gated_parts, axis=1)
    mixed_groups = jnp.concatenate(mixed_parts, axis=1)
    conv_local = jnp.stack(
        [jnp.concatenate(tap_zero, axis=0), jnp.concatenate(tap_one, axis=0)], axis=0
    )
    conv_total = lax.psum(conv_local, "fsdp")
    gated_time, mixed_time = (
        lax.all_to_all(gated_groups, "seq", split_axis=0, concat_axis=1, tiled=True),
        lax.all_to_all(mixed_groups, "seq", split_axis=0, concat_axis=1, tiled=True),
    )
    mixed_back = lax.dot_general(
        mixed_time,
        lax.all_gather(w_in, "fsdp", axis=0, tiled=True),
        (((1,), (1,)), ((), ())),
        preferred_element_type=jnp.float32,
    )
    grad_signal = (upstream.astype(jnp.float32) + mixed_back).astype(jnp.bfloat16)[None]
    gated_order = column_order(gated_time, fsdp_size, seq_size)
    record_order = column_order(record, fsdp_size, seq_size)
    part_out = lax.psum_scatter(
        outer_terms(gated_order, upstream), ("seq", "fsdp"), scatter_dimension=0, tiled=True
    )
    part_in = lax.psum_scatter(
        outer_terms(record_order, mixed_time), ("seq", "fsdp"), scatter_dimension=0, tiled=True
    )
    grad_in, grad_out = (
        lax.all_gather(part_in, "seq", axis=0, tiled=True),
        lax.all_gather(part_out, "seq", axis=0, tiled=True),
    )
    return (grad_signal, grad_in * factor, grad_out * factor, conv_total * factor)


def solution(mesh):
    placed = (
        P("fsdp", "seq", None),
        P("fsdp", "seq", None),
        P("fsdp", None),
        P(None, "seq", None),
        P("fsdp", None),
        P("seq"),
        P("fsdp"),
    )
    return jax.shard_map(
        local,
        mesh=mesh,
        in_specs=placed,
        out_specs=(P("fsdp", "seq", None), P("fsdp", None), P("fsdp", None), P(None, "seq", None)),
        check_vma=False,
    )
```

profile of v0, /device:TPU:0, one launch (start us, length us, event | category | flops | bytes accessed | tf_op | source)
XLA Modules:
  0.0 627.7 jit_solution(6793822717476289242)
XLA Ops:
  7.2 0.7 all-gather.7.cloned.1.call-update
  7.9 0.7 all-gather.5.cloned.1.call-update
  8.6 39.1 %all-gather.7.cloned.1.call-done = bf16[1024,1024]{1,0:T(8,128)(2,1)} async-done(((bf16[256,1024]{1,0:T(8,128)(2,1)}), bf16[1024,1024]{1,0:T(8,128)(2,1)}) %all-gather.7.cloned.1.call-update) | async-done | bytes 2097168 | tf_op jit(solution)/shard_map/all_gather | solution.py:67
  47.8 4.6 fusion.26
  52.4 2.4 copy.26
  54.7 4.6 all-to-all-start.1
  59.3 25.5 %all-gather.5.cloned.1.call-done = bf16[1024,1024]{1,0:T(8,128)(2,1)} async-done(((bf16[256,1024]{1,0:T(8,128)(2,1)}), bf16[1024,1024]{1,0:T(8,128)(2,1)}) %all-gather.5.cloned.1.call-update) | async-done | bytes 2097168 | tf_op jit(solution)/shard_map/all_gather | solution.py:71
  84.8 6.0 fusion.23
  90.8 17.6 %all-to-all-done.1 = bf16[1024,8,128]{2,0,1:T(8,128)(2,1)S(1)} async-done(((bf16[1024,8,128]{2,0,1:T(8,128)(2,1)}), bf16[1024,8,128]{2,0,1:T(8,128)(2,1)S(1)}, u32[]{:S(2)}, u32[]{:S(2)}) %all-to-all-start.1) | async-done | bytes 2097184 | tf_op jit(solution)/shard_map/all_to_all | solution.py:76
  108.4 4.7 all-to-all-start
  116.7 2.7 fusion.52
  119.4 42.5 %all-to-all-done = bf16[1024,8,128]{0,2,1:T(8,128)(2,1)} async-done(((bf16[1024,8,128]{0,2,1:T(8,128)(2,1)}), bf16[1024,8,128]{0,2,1:T(8,128)(2,1)}, u32[]{:S(2)}, u32[]{:S(2)}) %all-to-all-start) | async-done | bytes 2097184 | tf_op jit(solution)/shard_map/all_to_all | solution.py:77
  161.9 1.9 copy.42
  164.1 0.6 copy-done.1
  164.8 8.6 %pad_dynamic-slice_fusion.1 = (bf16[8192,64]{1,0:T(8,128)(2,1)S(1)}, bf16[8192,64]{1,0:T(8,128)(2,1)S(1)}) fusion(s32[]{:T(128)S(6)} %select_n.14, bf16[8192,64]{1,0:T(8,128)(2,1)S(1)} %copy-done, s32[]{:T(128)S(6)} %select_n.12, bf16[8192,64]{1,0:T(8,128)(2,1)S(1)} %copy-done.1), kind=kLoop, calls=%fused_computation.14 | loop fusion | bytes 4194312 | tf_op jit(solution)/shard_map/dynamic_slice | solution.py:10
  173.4 1.3 fusion.32
  174.8 0.6 copy-done.2
  175.4 1.5 fusion.30
  176.9 3.7 multiply_convert_fusion.3
  180.8 1.5 copy.45
  182.3 4.3 all-to-all-start.3
  190.3 3.1 pad_maximum_fusion.1
  193.4 42.3 %all-to-all-done.3 = bf16[8,1024,128]{1,2,0:T(8,128)(2,1)} async-done(((bf16[8,1024,128]{1,2,0:T(8,128)(2,1)}), bf16[8,1024,128]{1,2,0:T(8,128)(2,1)}, u32[]{:S(2)}, u32[]{:S(2)}) %all-to-all-start.3) | async-done | bytes 2097184 | tf_op jit(solution)/shard_map/all_to_all | solution.py:111
  235.7 1.9 copy.32
  237.9 4.3 fusion.19
  242.3 2.4 pad_dynamic-slice_fusion.2
  244.8 1.0 convolution_convert_fusion.1
  246.2 0.8 pad_dynamic-slice_fusion
  246.9 1.0 convolution_convert_fusion
  248.2 1.6 copy.46
  249.8 4.4 all-to-all-start.2
  254.2 4.0 copy.28
  258.2 3.3 copy.29
  261.4 49.1 %all-to-all-done.2 = bf16[8,1024,128]{1,2,0:T(8,128)(2,1)} async-done(((bf16[8,1024,128]{1,2,0:T(8,128)(2,1)}), bf16[8,1024,128]{1,2,0:T(8,128)(2,1)}, u32[]{:S(2)}, u32[]{:S(2)}) %all-to-all-start.2) | async-done | bytes 2097184 | tf_op jit(solution)/shard_map/all_to_all | solution.py:112
  310.5 6.6 %convolution_bitcast_fusion = f32[1024,1024]{0,1:T(8,128)} fusion(bf16[1024,1024]{0,1:T(8,128)(2,1)} %bitcast.20, bf16[1024,1024]{0,1:T(8,128)(2,1)} %bitcast.91), kind=kOutput, calls=%fused_computation.17 | convolution fusion | flops 2147483648 | bytes 8388608 | tf_op jit(solution)/shard_map/dot_general | solution.py:50
  317.1 5.5 copy.36
  323.0 4.5 fusion.31
  327.5 1.6 fusion.29
  329.2 0.7 pad_maximum_fusion.10
  329.9 56.5 %reduce-scatter.9.cloned.1.call-done = f32[32,1024]{1,0:T(8,128)} async-done(((f32[1024,1024]{1,0:T(8,128)}), f32[32,1024]{1,0:T(8,128)}) %reduce-scatter.9.cloned.1.call-update) | async-done | bytes 131088 | tf_op jit(solution)/shard_map/reduce_scatter | solution.py:123
  386.5 142.3 %reduce-scatter.7.cloned.1.call-done = f32[32,1024]{1,0:T(8,128)} async-done(((f32[1024,1024]{1,0:T(8,128)}), f32[32,1024]{1,0:T(8,128)}) %reduce-scatter.7.cloned.1.call-update) | async-done | bytes 131088 | tf_op jit(solution)/shard_map/reduce_scatter | solution.py:126
  528.8 42.5 %all-reduce.6.cloned.1.call-done = f32[2,128,128]{2,1,0:T(8,128)} async-done(((f32[2,128,128]{2,1,0:T(8,128)}), f32[2,128,128]{2,1,0:T(8,128)}) %all-reduce.6.cloned.1.call-update) | async-done | bytes 131088 | tf_op jit(solution)/shard_map/psum | solution.py:109
  571.3 1.6 broadcast_multiply_fusion.2
  572.9 6.6 %fusion.10 = bf16[1,1024,1024]{2,1,0:T(8,128)(2,1)} fusion(bf16[1,1024,1024]{2,1,0:T(8,128)(2,1)} %param.8, bf16[1024,1024]{0,1:T(8,128)(2,1)} %bitcast.20, bf16[1024,1024]{1,0:T(8,128)(2,1)} %all-gather.7.cloned.1.call-done), kind=kOutput, calls=%fused_computation.18 | convolution fusion | flops 2150629376 | bytes 8388608 | tf_op jit(solution)/shard_map/dot_general | solution.py:114
  579.5 15.6 %all-gather.11.cloned.1.call-done = f32[256,1024]{1,0:T(8,128)} async-done(((f32[32,1024]{1,0:T(8,128)}), f32[256,1024]{1,0:T(8,128)}) %all-gather.11.cloned.1.call-update) | async-done | bytes 1048592 | tf_op jit(solution)/shard_map/all_gather | solution.py:131
  595.1 2.3 broadcast_multiply_fusion
  597.4 21.1 %all-gather.9.cloned.1.call-done = f32[256,1024]{1,0:T(8,128)} async-done(((f32[32,1024]{1,0:T(8,128)}), f32[256,1024]{1,0:T(8,128)}) %all-gather.9.cloned.1.call-update) | async-done | bytes 1048592 | tf_op jit(solution)/shard_map/all_gather | solution.py:130
  618.5 2.3 broadcast_multiply_fusion.1
  (44 shorter events, 2.7 us)
Async XLA Ops:
  7.2 40.6 %all-gather.7.cloned.1.call-start = ((), (), s32[]{:S(2)}) async-start(), calls=%async_computation.7 | async-start | bytes 2621440 | tf_op jit(solution)/shard_map/all_gather | solution.py:67
  7.9 76.9 %all-gather.5.cloned.1.call-start = ((), (), s32[]{:S(2)}) async-start(), calls=%async_computation.6 | async-start | bytes 2621440 | tf_op jit(solution)/shard_map/all_gather | solution.py:71
  54.7 53.6 %all-to-all-start.1 = ((bf16[1024,8,128]{2,0,1:T(8,128)(2,1)}), bf16[1024,8,128]{2,0,1:T(8,128)(2,1)S(1)}, u32[]{:S(2)}, u32[]{:S(2)}) async-start(bf16[1024,8,128]{2,0,1:T(8,128)(2,1)} %copy.26), calls=%async_computation.1 | async-start | bytes 4194304 | tf_op jit(solution)/shard_map/all_to_all | solution.py:76
  108.4 4.7 copy-start.10
  108.4 8.3 %copy-start.9 = (bf16[2,128,128]{2,1,0:T(8,128)(2,1)S(1)}, bf16[2,128,128]{2,1,0:T(8,128)(2,1)}, u32[]{:S(2)}) copy-start(bf16[2,128,128]{2,1,0:T(8,128)(2,1)} %param.10) | copy-start | bytes 196612
  108.4 53.5 %all-to-all-start = ((bf16[1024,8,128]{0,2,1:T(8,128)(2,1)}), bf16[1024,8,128]{0,2,1:T(8,128)(2,1)}, u32[]{:S(2)}, u32[]{:S(2)}) async-start(bf16[1024,8,128]{0,2,1:T(8,128)(2,1)} %bitcast.90), calls=%async_computation | async-start | bytes 4194304 | tf_op jit(solution)/shard_map/all_to_all | solution.py:77
  161.9 2.2 copy-start
  161.9 2.9 copy-start.1
  173.4 1.4 copy-start.4
  173.4 2.0 copy-start.2
  182.3 53.4 %all-to-all-start.3 = ((bf16[8,1024,128]{1,2,0:T(8,128)(2,1)}), bf16[8,1024,128]{1,2,0:T(8,128)(2,1)}, u32[]{:S(2)}, u32[]{:S(2)}) async-start(bf16[8,1024,128]{1,2,0:T(8,128)(2,1)} %bitcast.84), calls=%async_computation.3 | async-start | bytes 4194304 | tf_op jit(solution)/shard_map/all_to_all | solution.py:111
  186.7 199.8 %reduce-scatter.9.cloned.1.call-start = ((), (), s32[]{:S(2)}) async-start(), calls=%async_computation.12 | async-start | bytes 4325376 | tf_op jit(solution)/shard_map/reduce_scatter | solution.py:123
  235.7 2.2 copy-start.11
  242.3 2.5 copy-start.7
  242.3 2.5 copy-start.8
  244.7 1.2 copy-start.5
  249.8 60.8 %all-to-all-start.2 = ((bf16[8,1024,128]{1,2,0:T(8,128)(2,1)}), bf16[8,1024,128]{1,2,0:T(8,128)(2,1)}, u32[]{:S(2)}, u32[]{:S(2)}) async-start(bf16[8,1024,128]{1,2,0:T(8,128)(2,1)} %bitcast.85), calls=%async_computation.2 | async-start | bytes 4194304 | tf_op jit(solution)/shard_map/all_to_all | solution.py:112
  254.1 274.7 %reduce-scatter.7.cloned.1.call-start = ((), (), s32[]{:S(2)}) async-start(), calls=%async_computation.11 | async-start | bytes 4325376 | tf_op jit(solution)/shard_map/reduce_scatter | solution.py:126
  322.7 248.7 %all-reduce.6.cloned.1.call-start = ((), (), s32[]{:S(2)}) async-start(), calls=%async_computation.10 | async-start | bytes 262144 | tf_op jit(solution)/shard_map/psum | solution.py:109
  323.0 4.5 copy-start.3
  323.0 4.5 copy-start.6
  329.9 265.2 %all-gather.11.cloned.1.call-start = ((), (), s32[]{:S(2)}) async-start(), calls=%async_computation.9 | async-start | bytes 1179648 | tf_op jit(solution)/shard_map/all_gather | solution.py:131
  386.5 232.0 %all-gather.9.cloned.1.call-start = ((), (), s32[]{:S(2)}) async-start(), calls=%async_computation.8 | async-start | bytes 1179648 | tf_op jit(solution)/shard_map/all_gather | solution.py:130
Sparse Core Ops, SparseCore 0:
  9.8 37.8 all-gather.6
  49.6 35.1 all-gather.4
  242.4 144.0 reduce-scatter.8
  388.6 140.1 reduce-scatter.6
  532.1 39.1 all-reduce.5
  572.8 22.2 all-gather.10
  596.7 21.8 all-gather.8
where the time goes:
time: 629 us; the launch traced here: 628 us
  waiting for transfers between devices  496 us (79%)
  local copies, waits for them, and re-layouts  39.4 us (6%)
  matrix products  38.9 us (6%)
  between operations  21 us (3%)
  starting transfers between devices  18.5 us (3%)
  other arithmetic  14.3 us (2%)
    reduce_scatter x1, waiting for transfers between devices, local(): lax.psum_scatter(outer_terms(record_order, mixed_time), ('seq', 'fsdp'),...  142 us
    reduce_scatter x1, waiting for transfers between devices, local(): lax.psum_scatter(outer_terms(gated_order, upstream), ('seq', 'fsdp'), sca...  56.5 us
    all_to_all x1, waiting for transfers between devices, local(): lax.all_to_all(mixed_groups, 'seq', split_axis=0, concat_axis=1, tiled=True)  49.1 us
    psum x1, waiting for transfers between devices, local(): conv_total = lax.psum(conv_local, 'fsdp')  42.5 us
    all_to_all x1, waiting for transfers between devices, local(): lax.all_to_all(grad_gated, 'seq', split_axis=1, concat_axis=0, tiled=True)  42.5 us
    all_to_all x1, waiting for transfers between devices, local(): lax.all_to_all(gated_groups, 'seq', split_axis=0, concat_axis=1, tiled=True)  42.3 us
    all_gather x1, waiting for transfers between devices, local(): lax.all_gather(w_in, 'fsdp', axis=0, tiled=True)  39.1 us
    all_gather x1, waiting for transfers between devices, local(): lax.all_gather(w_out, 'fsdp', axis=0, tiled=True)  25.5 us
  transfers between devices with their start and end apart: 11, of which 11 were waited for; matrix products, arithmetic and copies ran while one was open for 10% of the time, Pallas kernels for 0%

commit v1 on v0

--- a/solution.py
+++ b/solution.py
@@ -106,7 +106,11 @@
     conv_local = jnp.stack(
         [jnp.concatenate(tap_zero, axis=0), jnp.concatenate(tap_one, axis=0)], axis=0
     )
-    conv_total = lax.psum(conv_local, "fsdp")
+    conv_total = conv_local
+    for hop in (1, 2):
+        conv_total = conv_total + lax.ppermute(
+            conv_total, "fsdp", [(dev, dev ^ hop) for dev in range(4)]
+        )
     gated_time, mixed_time = (
         lax.all_to_all(gated_groups, "seq", split_axis=0, concat_axis=1, tiled=True),
         lax.all_to_all(mixed_groups, "seq", split_axis=0, concat_axis=1, tiled=True),

time: 629 us -> 582 us (0.925)
  waiting for transfers between devices: 496 us -> 451 us
    psum x1 -> x0, waiting for transfers between devices: 42.5 us -> none  [local(): conv_total = lax.psum(conv_local, 'fsdp')]
    all_gather x1, waiting for transfers between devices: 15.6 us -> 2.55 us  [local(): lax.all_gather(part_out, 'seq', axis=0, tiled=True)]
    ppermute x0 -> x2, waiting for transfers between devices: none -> 9.91 us  [local(): lax.ppermute(conv_total, 'fsdp', [(dev, dev ^ hop) for dev in range(4)])]
    reduce_scatter x1, waiting for transfers between devices: 56.5 us -> 63.7 us  [local(): lax.psum_scatter(outer_terms(gated_order, upstream), ('seq', 'fsdp'), sca...]
  transfers between devices with their start and end apart: 11 -> 12, of which waited for: 11 -> 12; matrix products, arithmetic and copies ran while one was open for 10% -> 11% of each run, Pallas kernels for 0% -> 0%
where the time goes in v1:
time: 582 us; the launch traced here: 581 us
  waiting for transfers between devices  451 us (77%)
  local copies, waits for them, and re-layouts  39.4 us (7%)
  matrix products  38.9 us (7%)
  between operations  21.2 us (4%)
  starting transfers between devices  18.6 us (3%)
  other arithmetic  12.8 us (2%)
    reduce_scatter x1, waiting for transfers between devices, local(): lax.psum_scatter(outer_terms(record_order, mixed_time), ('seq', 'fsdp'),...  136 us
    reduce_scatter x1, waiting for transfers between devices, local(): lax.psum_scatter(outer_terms(gated_order, upstream), ('seq', 'fsdp'), sca...  63.7 us
    all_to_all x1, waiting for transfers between devices, local(): lax.all_to_all(mixed_groups, 'seq', split_axis=0, concat_axis=1, tiled=True)  49.1 us
    all_to_all x1, waiting for transfers between devices, local(): lax.all_to_all(grad_gated, 'seq', split_axis=1, concat_axis=0, tiled=True)  42.4 us
    all_to_all x1, waiting for transfers between devices, local(): lax.all_to_all(gated_groups, 'seq', split_axis=0, concat_axis=1, tiled=True)  42.2 us
    all_gather x1, waiting for transfers between devices, local(): lax.all_gather(w_in, 'fsdp', axis=0, tiled=True)  39.1 us
    all_gather x1, waiting for transfers between devices, local(): lax.all_gather(w_out, 'fsdp', axis=0, tiled=True)  25.5 us
    all_gather x1, waiting for transfers between devices, local(): lax.all_gather(part_in, 'seq', axis=0, tiled=True)  21 us
  transfers between devices with their start and end apart: 12, of which 12 were waited for; matrix products, arithmetic and copies ran while one was open for 11% of the time, Pallas kernels for 0%

profile of v1, /device:TPU:0, one launch (start us, length us, event | category | flops | bytes accessed | tf_op | source)
XLA Modules:
  0.0 581.5 jit_solution(4977603245735271958)
XLA Ops:
  7.2 0.7 all-gather.7.cloned.1.call-update
  7.9 0.7 all-gather.5.cloned.1.call-update
  8.6 39.1 %all-gather.7.cloned.1.call-done = bf16[1024,1024]{1,0:T(8,128)(2,1)} async-done(((bf16[256,1024]{1,0:T(8,128)(2,1)}), bf16[1024,1024]{1,0:T(8,128)(2,1)}) %all-gather.7.cloned.1.call-update) | async-done | bytes 2097168 | tf_op jit(solution)/shard_map/all_gather | solution.py:67
  47.8 4.6 fusion.26
  52.4 2.4 copy.26
  54.7 4.6 all-to-all-start.1
  59.3 25.5 %all-gather.5.cloned.1.call-done = bf16[1024,1024]{1,0:T(8,128)(2,1)} async-done(((bf16[256,1024]{1,0:T(8,128)(2,1)}), bf16[1024,1024]{1,0:T(8,128)(2,1)}) %all-gather.5.cloned.1.call-update) | async-done | bytes 2097168 | tf_op jit(solution)/shard_map/all_gather | solution.py:71
  84.8 5.9 %fusion.23 = bf16[1024,1024]{0,1:T(8,128)(2,1)} fusion(bf16[1024,1024]{1,0:T(8,128)(2,1)} %all-gather.5.cloned.1.call-done, bf16[1,1024,1024]{2,1,0:T(8,128)(2,1)} %param.8), kind=kOutput, calls=%fused_computation.51 | convolution fusion | flops 2148532224 | bytes 6291456 | tf_op jit(solution)/shard_map/dot_general | solution.py:69
  90.7 17.6 %all-to-all-done.1 = bf16[1024,8,128]{2,0,1:T(8,128)(2,1)S(1)} async-done(((bf16[1024,8,128]{2,0,1:T(8,128)(2,1)}), bf16[1024,8,128]{2,0,1:T(8,128)(2,1)S(1)}, u32[]{:S(2)}, u32[]{:S(2)}) %all-to-all-start.1) | async-done | bytes 2097184 | tf_op jit(solution)/shard_map/all_to_all | solution.py:76
  108.4 4.7 all-to-all-start
  116.8 2.7 fusion.53
  119.5 42.4 %all-to-all-done = bf16[1024,8,128]{0,2,1:T(8,128)(2,1)} async-done(((bf16[1024,8,128]{0,2,1:T(8,128)(2,1)}), bf16[1024,8,128]{0,2,1:T(8,128)(2,1)}, u32[]{:S(2)}, u32[]{:S(2)}) %all-to-all-start) | async-done | bytes 2097184 | tf_op jit(solution)/shard_map/all_to_all | solution.py:77
  161.9 1.9 copy.42
  164.1 0.6 copy-done.1
  164.8 8.6 %pad_dynamic-slice_fusion.1 = (bf16[8192,64]{1,0:T(8,128)(2,1)S(1)}, bf16[8192,64]{1,0:T(8,128)(2,1)S(1)}) fusion(s32[]{:T(128)S(6)} %select_n.14, bf16[8192,64]{1,0:T(8,128)(2,1)S(1)} %copy-done, s32[]{:T(128)S(6)} %select_n.12, bf16[8192,64]{1,0:T(8,128)(2,1)S(1)} %copy-done.1), kind=kLoop, calls=%fused_computation.14 | loop fusion | bytes 4194312 | tf_op jit(solution)/shard_map/dynamic_slice | solution.py:10
  173.4 1.3 fusion.32
  174.8 0.6 copy-done.2
  175.4 1.5 fusion.30
  176.9 3.7 multiply_convert_fusion.3
  180.8 1.5 copy.45
  182.3 4.4 all-to-all-start.3
  190.4 3.1 pad_maximum_fusion.1
  193.5 42.2 %all-to-all-done.3 = bf16[8,1024,128]{1,2,0:T(8,128)(2,1)} async-done(((bf16[8,1024,128]{1,2,0:T(8,128)(2,1)}), bf16[8,1024,128]{1,2,0:T(8,128)(2,1)}, u32[]{:S(2)}, u32[]{:S(2)}) %all-to-all-start.3) | async-done | bytes 2097184 | tf_op jit(solution)/shard_map/all_to_all | solution.py:115
  235.7 1.9 copy.32
  237.9 4.3 fusion.19
  242.3 2.4 pad_dynamic-slice_fusion.2
  244.8 1.0 convolution_convert_fusion.1
  246.2 0.8 pad_dynamic-slice_fusion
  247.0 1.0 convolution_convert_fusion
  248.2 1.6 copy.46
  249.8 4.3 all-to-all-start.2
  254.2 4.0 copy.28
  258.1 3.3 copy.29
  261.4 49.1 %all-to-all-done.2 = bf16[8,1024,128]{1,2,0:T(8,128)(2,1)} async-done(((bf16[8,1024,128]{1,2,0:T(8,128)(2,1)}), bf16[8,1024,128]{1,2,0:T(8,128)(2,1)}, u32[]{:S(2)}, u32[]{:S(2)}) %all-to-all-start.2) | async-done | bytes 2097184 | tf_op jit(solution)/shard_map/all_to_all | solution.py:116
  310.5 6.6 %convolution_bitcast_fusion = f32[1024,1024]{0,1:T(8,128)} fusion(bf16[1024,1024]{0,1:T(8,128)(2,1)} %bitcast.20, bf16[1024,1024]{0,1:T(8,128)(2,1)} %bitcast.91), kind=kOutput, calls=%fused_computation.17 | convolution fusion | flops 2147483648 | bytes 8388608 | tf_op jit(solution)/shard_map/dot_general | solution.py:50
  317.2 5.5 copy.36
  322.7 63.7 %reduce-scatter.9.cloned.1.call-done = f32[32,1024]{1,0:T(8,128)} async-done(((f32[1024,1024]{1,0:T(8,128)}), f32[32,1024]{1,0:T(8,128)}) %reduce-scatter.9.cloned.1.call-update) | async-done | bytes 131088 | tf_op jit(solution)/shard_map/reduce_scatter | solution.py:127
  386.8 4.5 fusion.31
  391.3 1.6 fusion.29
  392.9 136.1 %reduce-scatter.7.cloned.1.call-done = f32[32,1024]{1,0:T(8,128)} async-done(((f32[1024,1024]{1,0:T(8,128)}), f32[32,1024]{1,0:T(8,128)}) %reduce-scatter.7.cloned.1.call-update) | async-done | bytes 131088 | tf_op jit(solution)/shard_map/reduce_scatter | solution.py:130
  529.1 5.0 collective-permute-done
  534.2 5.0 collective-permute-done.1
  539.1 0.7 add_multiply_fusion
  539.8 6.6 %fusion.10 = bf16[1,1024,1024]{2,1,0:T(8,128)(2,1)} fusion(bf16[1,1024,1024]{2,1,0:T(8,128)(2,1)} %param.8, bf16[1024,1024]{0,1:T(8,128)(2,1)} %bitcast.20, bf16[1024,1024]{1,0:T(8,128)(2,1)} %all-gather.7.cloned.1.call-done), kind=kOutput, calls=%fused_computation.18 | convolution fusion | flops 2150629376 | bytes 8388608 | tf_op jit(solution)/shard_map/dot_general | solution.py:118
  546.4 2.6 all-gather.11.cloned.1.call-done
  549.0 2.3 broadcast_multiply_fusion
  551.3 21.0 %all-gather.9.cloned.1.call-done = f32[256,1024]{1,0:T(8,128)} async-done(((f32[32,1024]{1,0:T(8,128)}), f32[256,1024]{1,0:T(8,128)}) %all-gather.9.cloned.1.call-update) | async-done | bytes 1048592 | tf_op jit(solution)/shard_map/all_gather | solution.py:134
  572.3 2.3 broadcast_multiply_fusion.1
  (46 shorter events, 2.8 us)
Async XLA Ops:
  7.2 40.6 %all-gather.7.cloned.1.call-start = ((), (), s32[]{:S(2)}) async-start(), calls=%async_computation.7 | async-start | bytes 2621440 | tf_op jit(solution)/shard_map/all_gather | solution.py:67
  7.9 76.9 %all-gather.5.cloned.1.call-start = ((), (), s32[]{:S(2)}) async-start(), calls=%async_computation.6 | async-start | bytes 2621440 | tf_op jit(solution)/shard_map/all_gather | solution.py:71
  54.7 53.6 %all-to-all-start.1 = ((bf16[1024,8,128]{2,0,1:T(8,128)(2,1)}), bf16[1024,8,128]{2,0,1:T(8,128)(2,1)S(1)}, u32[]{:S(2)}, u32[]{:S(2)}) async-start(bf16[1024,8,128]{2,0,1:T(8,128)(2,1)} %copy.26), calls=%async_computation.1 | async-start | bytes 4194304 | tf_op jit(solution)/shard_map/all_to_all | solution.py:76
  108.4 4.7 copy-start.10
  108.4 8.4 %copy-start.9 = (bf16[2,128,128]{2,1,0:T(8,128)(2,1)S(1)}, bf16[2,128,128]{2,1,0:T(8,128)(2,1)}, u32[]{:S(2)}) copy-start(bf16[2,128,128]{2,1,0:T(8,128)(2,1)} %param.10) | copy-start | bytes 196612
  108.4 53.5 %all-to-all-start = ((bf16[1024,8,128]{0,2,1:T(8,128)(2,1)}), bf16[1024,8,128]{0,2,1:T(8,128)(2,1)}, u32[]{:S(2)}, u32[]{:S(2)}) async-start(bf16[1024,8,128]{0,2,1:T(8,128)(2,1)} %bitcast.90), calls=%async_computation | async-start | bytes 4194304 | tf_op jit(solution)/shard_map/all_to_all | solution.py:77
  161.9 2.2 copy-start
  161.9 2.9 copy-start.1
  173.4 1.4 copy-start.4
  173.4 2.0 copy-start.2
  182.3 53.4 %all-to-all-start.3 = ((bf16[8,1024,128]{1,2,0:T(8,128)(2,1)}), bf16[8,1024,128]{1,2,0:T(8,128)(2,1)}, u32[]{:S(2)}, u32[]{:S(2)}) async-start(bf16[8,1024,128]{1,2,0:T(8,128)(2,1)} %bitcast.84), calls=%async_computation.3 | async-start | bytes 4194304 | tf_op jit(solution)/shard_map/all_to_all | solution.py:115
  186.7 199.7 %reduce-scatter.9.cloned.1.call-start = ((), (), s32[]{:S(2)}) async-start(), calls=%async_computation.11 | async-start | bytes 4325376 | tf_op jit(solution)/shard_map/reduce_scatter | solution.py:127
  235.7 2.2 copy-start.11
  242.3 2.5 copy-start.7
  242.3 2.5 copy-start.8
  244.8 1.2 copy-start.5
  249.8 60.8 %all-to-all-start.2 = ((bf16[8,1024,128]{1,2,0:T(8,128)(2,1)}), bf16[8,1024,128]{1,2,0:T(8,128)(2,1)}, u32[]{:S(2)}, u32[]{:S(2)}) async-start(bf16[8,1024,128]{1,2,0:T(8,128)(2,1)} %bitcast.85), calls=%async_computation.2 | async-start | bytes 4194304 | tf_op jit(solution)/shard_map/all_to_all | solution.py:116
  254.1 274.9 %reduce-scatter.7.cloned.1.call-start = ((), (), s32[]{:S(2)}) async-start(), calls=%async_computation.10 | async-start | bytes 4325376 | tf_op jit(solution)/shard_map/reduce_scatter | solution.py:130
  322.7 226.3 %all-gather.11.cloned.1.call-start = ((), (), s32[]{:S(2)}) async-start(), calls=%async_computation.9 | async-start | bytes 1179648 | tf_op jit(solution)/shard_map/all_gather | solution.py:135
  386.5 185.8 %all-gather.9.cloned.1.call-start = ((), (), s32[]{:S(2)}) async-start(), calls=%async_computation.8 | async-start | bytes 1179648 | tf_op jit(solution)/shard_map/all_gather | solution.py:134
  386.8 4.5 copy-start.3
  386.8 4.5 copy-start.6
  529.0 5.0 collective-permute-start
  534.1 5.0 collective-permute-start.1
Sparse Core Ops, SparseCore 0:
  9.8 37.8 all-gather.6
  49.6 35.1 all-gather.4
  242.4 143.9 reduce-scatter.8
  388.6 140.3 reduce-scatter.6
  530.4 18.4 all-gather.10
  550.4 21.8 all-gather.8
